TPU v7x, 128 devices: a whole 4x4x4 slice. The times are simulated.
128 devices in a mesh: blk: 32 (over x_hi, z, y), grp: 4 (over x_lo, core).
Axes of the slice: x: 4 (x_hi: 2, x_lo: 2; x = x_hi * 2 + x_lo), y: 4, z: 4, core: 2. Of those that a mesh axis runs over, the one named last changes fastest.
Arguments:
- images: bfloat16 [8192, 1536], P('blk'), may hold values from -100 to 100
- defocus: float32 [8192], P('blk'), may hold values from 1 to 12
- class_id: int32 [8192, 1], P('blk'), may hold values from 0 to 255; in each aligned block of 256 rows (0 to 255, 256 to 511, ...) at most 2 rows name the same one
- rotation_id: int32 [8192], P('blk'), may hold values from 0 to 31
- shift_id: int32 [8192], P('blk'), may hold values from 0 to 8
- references: float32 [4, 64, 1536], P('grp', 'blk'), may hold values from -4 to 4
- owner: int32 [4, 64], P('grp'), may hold values from 0 to 63, as said below
- inv_noise: float32 [24], replicated, may hold values from 0.5 to 2
- prior: float32 [24], replicated, may hold values from 0.5 to 2
Outputs:
- evidence: float32 [8192], P('blk')
- new_refs: float32 [4, 64, 1536], P('grp', 'blk')
Inputs may be any that keep to these rules, and one draw needn't show every extreme that they name: `class_id`: among the particles of one index of blk, no class is assigned to more than 2 particles, and some class to exactly 2. `owner`: each row is a permutation of 0 to 63.
All inputs are finite; a program needn't handle non-finite values.
Results may differ from a plain program's by a relative error of at most 0.0036.
Values sent between devices are 32-bit elements; how exact they have to be, the bound alone decides.
No kernel may reach another device: no remote copies, remote signals or barrier semaphores. Data moves between devices by JAX's collectives and lax.ppermute only.
A program may use at most 64 MiB of HBM per device.

v0:
```python
import math
import jax
import jax.numpy as jnp
from jax import lax
from jax.sharding import PartitionSpec as P

CYCLES = 24
ANGLES = 32
SHIFTS = 9
CL_DEV = 2


def contrast_table(defocus):
    frequency = (jnp.arange(CYCLES, dtype=jnp.float32) + 1.0) / CYCLES
    return -jnp.sin(defocus[:, None] * (frequency * frequency)[None, :] + 0.15)


def phase_tables():
    radius = (jnp.arange(CYCLES, dtype=jnp.float32) + 1.0) / (2.0 * CYCLES)
    bearing = 2.0 * math.pi / ANGLES * jnp.arange(ANGLES, dtype=jnp.float32)
    shift_index = jnp.arange(SHIFTS, dtype=jnp.int32)
    shift_x = (shift_index // 3 - 1).astype(jnp.float32)
    shift_y = (shift_index % 3 - 1).astype(jnp.float32)
    along = (
        shift_x[:, None] * jnp.cos(bearing)[None, :] + shift_y[:, None] * jnp.sin(bearing)[None, :]
    )
    phase = -2.0 * math.pi * radius[None, :, None] * along[:, None, :]
    return (jnp.cos(phase), jnp.sin(phase))


def weigh(images, factor):
    row_total = images.shape[0]
    grid = images.astype(jnp.float32).reshape(row_total, 2, CYCLES, ANGLES)
    return (grid * factor[:, None, :, None]).reshape(row_total, -1).astype(jnp.bfloat16)


def make_templates(ref_block):
    block_rows = ref_block.shape[0]
    grid = ref_block.reshape(block_rows, 2, CYCLES, ANGLES)
    angular = jnp.arange(ANGLES, dtype=jnp.int32)
    turning = (
        angular[:, None, None] == (angular[None, None, :] - angular[None, :, None]) % ANGLES
    ).astype(jnp.float32)
    rotated = jnp.einsum("nqka,arb->nrqkb", grid, turning, precision=lax.Precision.HIGHEST)
    phase_cos, phase_sin = phase_tables()
    rotated_re = rotated[:, :, 0][:, :, None]
    rotated_im = rotated[:, :, 1][:, :, None]
    real_part = phase_cos[None, None] * rotated_re - phase_sin[None, None] * rotated_im
    imag_part = phase_sin[None, None] * rotated_re + phase_cos[None, None] * rotated_im
    stacked = jnp.stack([real_part, imag_part], axis=3)
    return stacked.reshape(block_rows * ANGLES * SHIFTS, -1).astype(jnp.bfloat16)


def score_block(ref_block, weighted, contrast_power, score_scale):
    block_rows = ref_block.shape[0]
    templates = make_templates(ref_block)
    cross = lax.dot_general(
        templates, weighted, (((1,), (1,)), ((), ())), preferred_element_type=jnp.float32
    )
    grid = ref_block.reshape(block_rows, 2, CYCLES, ANGLES)
    power = jnp.sum(grid * grid, axis=(1, 3))
    penalty = jnp.dot(power, contrast_power.T, precision=lax.Precision.HIGHEST)
    logits = (
        cross.reshape(block_rows, ANGLES * SHIFTS, -1) - 0.5 * penalty[:, None, :]
    ) * score_scale
    return logits.reshape(block_rows * ANGLES * SHIFTS, -1)


def target_rows(relative, rotation_id, shift_id):
    inside = (relative >= 0) & (relative < CL_DEV)
    return jnp.where(inside, (relative * ANGLES + rotation_id) * SHIFTS + shift_id, -1)


def update(running, logits, target):
    peak, total, picked = running
    new_peak = jnp.maximum(peak, jnp.max(logits, axis=0))
    total = total * jnp.exp(peak - new_peak) + jnp.sum(jnp.exp(logits - new_peak[None, :]), axis=0)
    row_index = jnp.arange(logits.shape[0], dtype=jnp.int32)
    picked = picked + jnp.sum(jnp.where(row_index[:, None] == target[None, :], logits, 0.0), axis=0)
    return (new_peak, total, picked)


def align_terms(images, contrast, weight, rotation_id, shift_id):
    row_total = images.shape[0]
    phase_cos, phase_sin = phase_tables()
    chosen = (shift_id[:, None] == jnp.arange(SHIFTS, dtype=jnp.int32)[None, :]).astype(jnp.float32)
    cos_rows = jnp.dot(
        chosen, phase_cos.reshape(SHIFTS, -1), precision=lax.Precision.HIGHEST
    ).reshape(row_total, CYCLES, ANGLES)
    sin_rows = jnp.dot(
        chosen, phase_sin.reshape(SHIFTS, -1), precision=lax.Precision.HIGHEST
    ).reshape(row_total, CYCLES, ANGLES)
    grid = images.astype(jnp.float32).reshape(row_total, 2, CYCLES, ANGLES)
    unshift_re = cos_rows * grid[:, 0] + sin_rows * grid[:, 1]
    unshift_im = cos_rows * grid[:, 1] - sin_rows * grid[:, 0]
    unshifted = jnp.stack([unshift_re, unshift_im], axis=1)
    angular = jnp.arange(ANGLES, dtype=jnp.int32)
    turning = (
        angular[None, :, None] == (angular[None, None, :] + rotation_id[:, None, None]) % ANGLES
    ).astype(jnp.float32)
    aligned = jnp.einsum("pqka,pab->pqkb", unshifted, turning, precision=lax.Precision.HIGHEST)
    scaled = weight[:, None] * contrast
    numer_term = (aligned * scaled[:, None, :, None]).reshape(row_total, -1)
    denom_term = weight[:, None] * contrast * contrast
    return (numer_term, denom_term)


def finish(numerator, denominator, prior):
    grid = numerator.reshape(-1, 2, CYCLES, ANGLES)
    return (grid / (denominator + prior[None, :])[:, None, :, None]).reshape(numerator.shape)


def shards(images, defocus, class_id, rotation_id, shift_id, references, owner, inv_noise, prior):
    particle_count = images.shape[0]
    group_classes = owner.shape[1]
    class_total = group_classes * lax.axis_size("grp")
    contrast = contrast_table(defocus)
    contrast_power = contrast * contrast * inv_noise[None, :]
    weighted = weigh(images, contrast * inv_noise[None, :])
    score_scale = 1.0 / math.sqrt(images.shape[1])
    local_class = class_id[:, 0] - lax.axis_index("grp") * group_classes
    member = (local_class >= 0) & (local_class < group_classes)
    initial = (
        jnp.full((particle_count,), -1e30, jnp.float32),
        jnp.zeros((particle_count,), jnp.float32),
        jnp.zeros((particle_count,), jnp.float32),
    )
    running = initial
    shard_piece = lax.all_gather(references, "blk", axis=1, tiled=True)
    blocks = shard_piece[0].reshape(-1, CL_DEV, shard_piece.shape[2])
    firsts = CL_DEV * jnp.arange(blocks.shape[0], dtype=jnp.int32)

    def advance(running_state, entries):
        ref_block, block_first = entries
        logits = score_block(ref_block, weighted, contrast_power, score_scale)
        return (
            update(
                running_state, logits, target_rows(local_class - block_first, rotation_id, shift_id)
            ),
            None,
        )

    running, unused = lax.scan(advance, running, (blocks, firsts))
    peak, total, picked = running
    global_peak = lax.pmax(peak, "grp")
    global_total = lax.psum(total * jnp.exp(peak - global_peak), "grp")
    log_sum = global_peak + jnp.log(global_total)
    log_orients = math.log(class_total * ANGLES * SHIFTS)
    evidence = log_sum - log_orients
    weight = jnp.where(member, jnp.exp(jnp.where(member, picked - log_sum + log_orients, 0.0)), 0.0)
    numer_term, denom_term = align_terms(images, contrast, weight, rotation_id, shift_id)
    safe_class = jnp.where(member, local_class, 0)
    class_index = jnp.arange(group_classes, dtype=jnp.int32)
    slot = jnp.sum(
        jnp.where(safe_class[:, None] == class_index[None, :], owner[0][None, :], 0), axis=1
    )
    owning = (class_index[:, None] == jnp.where(member, slot, -1)[None, :]).astype(jnp.float32)
    partial_numer = jnp.dot(owning, numer_term, precision=lax.Precision.HIGHEST)
    partial_denom = jnp.dot(owning, denom_term, precision=lax.Precision.HIGHEST)
    numerator, denominator = (
        lax.psum_scatter(partial_numer, "blk", scatter_dimension=0, tiled=True),
        lax.psum_scatter(partial_denom, "blk", scatter_dimension=0, tiled=True),
    )
    new_refs = finish(numerator, denominator, prior)[None]
    return (evidence, new_refs)


def solution(mesh):
    in_specs = (
        P("blk", None),
        P("blk"),
        P("blk", None),
        P("blk"),
        P("blk"),
        P("grp", "blk", None),
        P("grp", None),
        P(),
        P(),
    )
    out_specs = (P("blk"), P("grp", "blk", None))
    return jax.shard_map(shards, mesh=mesh, in_specs=in_specs, out_specs=out_specs, check_vma=False)
```

profile of v0, /device:TPU:6, one launch (start us, length us, event | category | flops | bytes accessed | tf_op | source)
XLA Modules:
  0.0 1281.5 jit_solution(13221657645334171205)
XLA Ops:
  10.8 96.7 %all_gather.3 = f32[1,64,1536]{2,0,1:T(1,128)S(1)} all-gather(f32[1,2,1536]{2,0,1:T(1,128)S(1)} %copy.46), channel_id=1, replica_groups=mesh['blk'=32,'grp'=4] {'blk'}, dimensions={1}, use_global_device_ids=true | all-gather | bytes 405504 | tf_op jit(solution)/shard_map/all_gather | solution.py:129
  113.6 786.5 %while.18 = (s32[]{:T(128)}, f32[256]{0:T(256)S(1)}, f32[256]{0:T(256)}, f32[256]{0:T(256)}, f32[32,2,1536]{2,1,0:T(2,128)S(1)}, /*index=5*/bf16[256,1536]{1,0:T...) while((s32[]{:T(128)}, f32[256]{0:T(256)S(1)}, ...), condition=%wide.region_5.6_spmd.clone, body=%wide.region_0.5_spmd.clone.sunk | while | flops 496573632 | bytes 14409568 | solution.py:143
  119.1 4.4 pad_maximum_fusion.3
  123.5 8.9 convert_element_type.90
  143.0 4.4 pad_maximum_fusion.3
  147.4 8.9 convert_element_type.90
  167.7 4.4 pad_maximum_fusion.3
  172.0 8.9 convert_element_type.90
  192.2 4.4 pad_maximum_fusion.3
  196.6 8.9 convert_element_type.90
  216.8 4.4 pad_maximum_fusion.3
  221.2 8.9 convert_element_type.90
  241.4 4.4 pad_maximum_fusion.3
  245.8 8.9 convert_element_type.90
  266.0 4.4 pad_maximum_fusion.3
  270.4 8.9 convert_element_type.90
  290.6 4.4 pad_maximum_fusion.3
  295.0 8.9 convert_element_type.90
  315.2 4.4 pad_maximum_fusion.3
  319.6 8.9 convert_element_type.90
  339.8 4.4 pad_maximum_fusion.3
  344.2 8.9 convert_element_type.90
  364.4 4.4 pad_maximum_fusion.3
  368.8 8.9 convert_element_type.90
  389.0 4.4 pad_maximum_fusion.3
  393.4 8.9 convert_element_type.90
  413.6 4.4 pad_maximum_fusion.3
  418.0 8.9 convert_element_type.90
  438.2 4.4 pad_maximum_fusion.3
  442.6 8.9 convert_element_type.90
  462.8 4.4 pad_maximum_fusion.3
  467.2 8.9 convert_element_type.90
  487.4 4.4 pad_maximum_fusion.3
  491.8 8.9 convert_element_type.90
  512.0 4.4 pad_maximum_fusion.3
  516.4 8.9 convert_element_type.90
  536.6 4.4 pad_maximum_fusion.3
  541.0 8.9 convert_element_type.90
  565.6 8.9 convert_element_type.90
  585.8 4.4 pad_maximum_fusion.3
  590.2 8.9 convert_element_type.90
  610.4 4.4 pad_maximum_fusion.3
  614.8 8.9 convert_element_type.90
  639.4 8.9 convert_element_type.90
  664.0 8.9 convert_element_type.90
  684.2 4.4 pad_maximum_fusion.3
  688.6 8.9 convert_element_type.90
  713.2 8.9 convert_element_type.90
  737.8 8.9 convert_element_type.90
  762.4 8.9 convert_element_type.90
  782.6 4.4 pad_maximum_fusion.3
  787.0 8.9 convert_element_type.90
  811.6 8.9 convert_element_type.90
  836.2 8.9 convert_element_type.90
  860.8 8.9 convert_element_type.90
  881.0 4.4 pad_maximum_fusion.3
  885.3 8.9 convert_element_type.90
  900.1 5.7 pmax.7
  906.5 5.9 psum.7
  918.9 5.2 copy.51
  924.1 7.6 broadcast_multiply_fusion
  931.7 5.1 copy.53
  940.7 176.2 %all-reduce.1 = f32[64,24]{1,0:T(8,128)S(1)} all-reduce(f32[64,24]{1,0:T(8,128)S(1)} %fusion.44), channel_id=3, replica_groups=mesh['blk'=32,'grp'=4] {'blk'}, use_global_device_ids=true, to_apply=%region_10.11.clone | all-reduce | flops 1536 | bytes 12288
  1117.1 156.1 %all-reduce.4.cloned.1.call-done = f32[64,1536]{1,0:T(8,128)} async-done(((f32[64,1536]{1,0:T(8,128)}), f32[64,1536]{1,0:T(8,128)}) %all-reduce.4.cloned.1.call-update) | async-done | bytes 393232
  (897 shorter events, 419.9 us)
Async XLA Ops:
  7.2 105.1 %copy-start.2 = (s32[256]{0:T(256)S(1)}, s32[256]{0:T(256)}, u32[]{:S(2)}) copy-start(s32[256]{0:T(256)} %param.14) | copy-start | bytes 3076
  7.2 105.8 %copy-start.3 = (s32[256,1]{0,1:T(1,128)S(1)}, s32[256,1]{0,1:T(1,128)}, u32[]{:S(2)}) copy-start(s32[256,1]{0,1:T(1,128)} %param.13) | copy-start | bytes 3076
  7.2 106.4 %copy-start.1 = (s32[256]{0:T(256)S(1)}, s32[256]{0:T(256)}, u32[]{:S(2)}) copy-start(s32[256]{0:T(256)} %param.15) | copy-start | bytes 3076
  7.2 1266.0 %all-reduce.4.cloned.1.call-start = ((), (), s32[]{:S(2)}) async-start(), calls=%async_computation | async-start | bytes 786432
  132.4 2.4 copy-start.6
  156.3 2.4 copy-start.6
  180.9 2.4 copy-start.6
  205.5 2.4 copy-start.6
  230.1 2.4 copy-start.6
  254.7 2.4 copy-start.6
  279.3 2.4 copy-start.6
  303.9 2.4 copy-start.6
  328.5 2.4 copy-start.6
  353.1 2.4 copy-start.6
  377.7 2.4 copy-start.6
  402.3 2.4 copy-start.6
  426.9 2.4 copy-start.6
  451.5 2.4 copy-start.6
  476.1 2.4 copy-start.6
  500.7 2.4 copy-start.6
  525.3 2.4 copy-start.6
  549.9 2.4 copy-start.6
  574.5 2.4 copy-start.6
  599.1 2.4 copy-start.6
  623.7 2.4 copy-start.6
  648.3 2.4 copy-start.6
  672.9 2.4 copy-start.6
  697.5 2.4 copy-start.6
  722.1 2.4 copy-start.6
  746.7 2.4 copy-start.6
  771.3 2.4 copy-start.6
  795.9 2.4 copy-start.6
  820.5 2.4 copy-start.6
  845.1 2.4 copy-start.6
  869.7 2.4 copy-start.6
  894.3 2.4 copy-start.6
  918.9 5.2 copy-start
  931.7 6.8 copy-start.5
  931.7 185.3 %copy-start.4 = (f32[24]{0:T(128)S(1)}, f32[24]{0:T(128)}, u32[]{:S(2)}) copy-start(f32[24]{0:T(128)} %param.19) | copy-start | bytes 292
Sparse Core Ops, SparseCore 0:
  938.6 334.5 all-reduce.3
where the time goes:
time: 1290 us; the launch traced here: 1280 us
  other arithmetic  331 us (26%)
  local copies, waits for them, and re-layouts  329 us (26%)
  blocking collectives  285 us (22%)
  matrix products  163 us (13%)
  waiting for transfers between devices  156 us (12%)
  between operations  14.9 us (1%)
    convert_element_type x32, local copies, waits for them, and re-layouts, make_templates(): stacked.reshape(block_rows * ANGLES * SHIFTS, -1).astype(jnp.bfloat16)  285 us
    unnamed x1, blocking collectives  176 us
    unnamed x2, waiting for transfers between devices  156 us
    another operation x32, other arithmetic, make_templates(): stacked = jnp.stack([real_part, imag_part], axis=3)  139 us
    all_gather x1, blocking collectives, shards(): shard_piece = lax.all_gather(references, 'blk', axis=1, tiled=True)  96.7 us
    dot_general x32, matrix products, score_block(): lax.dot_general(templates, weighted, (((1,), (1,)), ((), ())), preferred_...  76.6 us
    another operation x32, other arithmetic  65.7 us
    dot_general x32, matrix products, score_block(): penalty = jnp.dot(power, contrast_power.T, precision=lax.Precision.HIGHEST)  50.4 us
  transfers between devices with their start and end apart: 1, of which 1 were waited for; matrix products, arithmetic and copies ran while one was open for 0% of the time, Pallas kernels for 0%

commit v1 on v0

--- a/solution.py
+++ b/solution.py
@@ -8,6 +8,11 @@
 ANGLES = 32
 SHIFTS = 9
 CL_DEV = 2
+
+
+def exchange_gather(shard, axis, dim):
+    outgoing = jnp.stack([shard] * lax.axis_size(axis))
+    return jnp.concatenate(lax.all_to_all(outgoing, axis, 0, 0), axis=dim)
 
 
 def contrast_table(defocus):
@@ -126,7 +131,7 @@
         jnp.zeros((particle_count,), jnp.float32),
     )
     running = initial
-    shard_piece = lax.all_gather(references, "blk", axis=1, tiled=True)
+    shard_piece = exchange_gather(references, "blk", 1)
     blocks = shard_piece[0].reshape(-1, CL_DEV, shard_piece.shape[2])
     firsts = CL_DEV * jnp.arange(blocks.shape[0], dtype=jnp.int32)
 

time: 1290 us -> 1190 us (0.922)
  blocking collectives: 285 us -> 193 us
  matrix products: 163 us -> 148 us
    all_gather x1 -> x0, blocking collectives: 96.7 us -> none  [shards(): shard_piece = lax.all_gather(references, 'blk', axis=1, tiled=True)]
    dot_general x32, matrix products: 76.6 us -> 61.6 us  [score_block(): lax.dot_general(templates, weighted, (((1,), (1,)), ((), ())), preferred_...]
  transfers between devices with their start and end apart: 1 -> 2, of which waited for: 1 -> 1; matrix products, arithmetic and copies ran while one was open for 0% -> 1% of each run, Pallas kernels for 0% -> 0%
where the time goes in v1:
time: 1190 us; the launch traced here: 1180 us
  local copies, waits for them, and re-layouts  329 us (28%)
  other arithmetic  327 us (27%)
  blocking collectives  193 us (16%)
  waiting for transfers between devices  157 us (13%)
  matrix products  148 us (12%)
  between operations  14.9 us (1%)
    convert_element_type x32, local copies, waits for them, and re-layouts, make_templates(): stacked.reshape(block_rows * ANGLES * SHIFTS, -1).astype(jnp.bfloat16)  285 us
    unnamed x1, blocking collectives  181 us
    unnamed x2, waiting for transfers between devices  157 us
    another operation x32, other arithmetic, make_templates(): stacked = jnp.stack([real_part, imag_part], axis=3)  139 us
    another operation x32, other arithmetic  65.7 us
    dot_general x32, matrix products, score_block(): lax.dot_general(templates, weighted, (((1,), (1,)), ((), ())), preferred_...  61.6 us
    dot_general x32, matrix products, score_block(): penalty = jnp.dot(power, contrast_power.T, precision=lax.Precision.HIGHEST)  50.4 us
    add x32, other arithmetic, update(): picked + jnp.sum(jnp.where(row_index[:, None] == target[None, :], logits,...  39.7 us
  transfers between devices with their start and end apart: 2, of which 1 were waited for; matrix products, arithmetic and copies ran while one was open for 1% of the time, Pallas kernels for 0%

profile of v1, /device:TPU:6, one launch (start us, length us, event | category | flops | bytes accessed | tf_op | source)
XLA Modules:
  0.0 1183.2 jit_solution(6022857745491484745)
XLA Ops:
  8.8 11.1 all-to-all-start
  28.3 5.4 copy.48
  36.3 770.0 %while.18 = (s32[]{:T(128)}, f32[256]{0:T(256)S(1)}, f32[256]{0:T(256)}, f32[256]{0:T(256)}, f32[32,2,1536]{2,1,0:T(2,128)S(1)}, /*index=5*/bf16[256,1536]{1,0:T...) while((s32[]{:T(128)}, f32[256]{0:T(256)S(1)}, ...), condition=%wide.region_5.6_spmd.clone, body=%wide.region_0.5_spmd.clone.sunk | while | flops 496573632 | bytes 14409568 | solution.py:148
  41.8 4.4 pad_maximum_fusion.3
  46.1 8.9 convert_element_type.90
  65.2 4.4 pad_maximum_fusion.3
  69.5 8.9 convert_element_type.90
  89.3 4.4 pad_maximum_fusion.3
  93.6 8.9 convert_element_type.90
  113.4 4.4 pad_maximum_fusion.3
  117.7 8.9 convert_element_type.90
  137.4 4.4 pad_maximum_fusion.3
  141.8 8.9 convert_element_type.90
  161.5 4.4 pad_maximum_fusion.3
  165.9 8.9 convert_element_type.90
  185.6 4.4 pad_maximum_fusion.3
  190.0 8.9 convert_element_type.90
  209.7 4.4 pad_maximum_fusion.3
  214.0 8.9 convert_element_type.90
  233.8 4.4 pad_maximum_fusion.3
  238.1 8.9 convert_element_type.90
  257.9 4.4 pad_maximum_fusion.3
  262.2 8.9 convert_element_type.90
  281.9 4.4 pad_maximum_fusion.3
  286.3 8.9 convert_element_type.90
  306.0 4.4 pad_maximum_fusion.3
  310.4 8.9 convert_element_type.90
  330.1 4.4 pad_maximum_fusion.3
  334.5 8.9 convert_element_type.90
  354.2 4.4 pad_maximum_fusion.3
  358.5 8.9 convert_element_type.90
  382.6 8.9 convert_element_type.90
  402.4 4.4 pad_maximum_fusion.3
  406.7 8.9 convert_element_type.90
  430.8 8.9 convert_element_type.90
  450.5 4.4 pad_maximum_fusion.3
  454.9 8.9 convert_element_type.90
  479.0 8.9 convert_element_type.90
  498.7 4.4 pad_maximum_fusion.3
  503.1 8.9 convert_element_type.90
  527.1 8.9 convert_element_type.90
  546.9 4.4 pad_maximum_fusion.3
  551.2 8.9 convert_element_type.90
  575.3 8.9 convert_element_type.90
  595.0 4.4 pad_maximum_fusion.3
  599.4 8.9 convert_element_type.90
  623.5 8.9 convert_element_type.90
  643.2 4.4 pad_maximum_fusion.3
  647.6 8.9 convert_element_type.90
  671.6 8.9 convert_element_type.90
  691.4 4.4 pad_maximum_fusion.3
  695.7 8.9 convert_element_type.90
  715.5 4.4 pad_maximum_fusion.3
  719.8 8.9 convert_element_type.90
  743.9 8.9 convert_element_type.90
  763.6 4.4 pad_maximum_fusion.3
  768.0 8.9 convert_element_type.90
  792.1 8.9 convert_element_type.90
  806.3 5.6 pmax.7
  812.6 6.4 psum.7
  821.2 7.6 broadcast_multiply_fusion
  828.8 5.1 copy.50
  836.6 181.3 %all-reduce.1 = f32[64,24]{1,0:T(8,128)S(1)} all-reduce(f32[64,24]{1,0:T(8,128)S(1)} %fusion.44), channel_id=3, replica_groups=mesh['blk'=32,'grp'=4] {'blk'}, use_global_device_ids=true, to_apply=%region_10.11.clone | all-reduce | flops 1536 | bytes 12288
  1018.1 156.9 %all-reduce.4.cloned.1.call-done = f32[64,1536]{1,0:T(8,128)} async-done(((f32[64,1536]{1,0:T(8,128)}), f32[64,1536]{1,0:T(8,128)}) %all-reduce.4.cloned.1.call-update) | async-done | bytes 393232
  (900 shorter events, 400.8 us)
Async XLA Ops:
  7.2 15.6 %copy-start.4 = (s32[256,1]{0,1:T(1,128)S(1)}, s32[256,1]{0,1:T(1,128)}, u32[]{:S(2)}) copy-start(s32[256,1]{0,1:T(1,128)} %param.13) | copy-start | bytes 3076
  7.2 15.6 %copy-start.5 = (s32[1,64]{1,0:T(1,128)S(1)}, s32[1,64]{1,0:T(1,128)}, u32[]{:S(2)}) copy-start(s32[1,64]{1,0:T(1,128)} %param.17) | copy-start | bytes 772
  7.2 16.3 %copy-start.1 = (s32[256]{0:T(256)S(1)}, s32[256]{0:T(256)}, u32[]{:S(2)}) copy-start(s32[256]{0:T(256)} %param.15) | copy-start | bytes 3076
  8.8 27.5 %all-to-all-start = ((f32[32,1,2,1536]{3,2,1,0:T(2,128)}), f32[32,1,2,1536]{3,2,1,0:T(2,128)S(1)}, u32[]{:S(2)}, u32[]{:S(2)}) async-start(f32[32,1,2,1536]{3,2,1,0:T(2,128)} %stack.15), calls=%async_computation | async-start | bytes 786432 | tf_op jit(solution)/shard_map/all_to_all | solution.py:15
  19.8 1155.2 %all-reduce.4.cloned.1.call-start = ((), (), s32[]{:S(2)}) async-start(), calls=%async_computation.1 | async-start | bytes 786432
  28.3 5.4 copy-start.8
  28.3 7.2 copy-start.2
  28.3 8.0 copy-start
  55.1 1.9 copy-start.7
  78.5 1.9 copy-start.7
  102.6 1.9 copy-start.7
  126.6 1.9 copy-start.7
  150.7 1.9 copy-start.7
  174.8 1.9 copy-start.7
  198.9 1.9 copy-start.7
  223.0 1.9 copy-start.7
  247.1 1.9 copy-start.7
  271.1 1.9 copy-start.7
  295.2 1.9 copy-start.7
  319.3 1.9 copy-start.7
  343.4 1.9 copy-start.7
  367.5 1.9 copy-start.7
  391.6 1.9 copy-start.7
  415.6 1.9 copy-start.7
  439.7 1.9 copy-start.7
  463.8 1.9 copy-start.7
  487.9 1.9 copy-start.7
  512.0 1.9 copy-start.7
  536.1 1.9 copy-start.7
  560.1 1.9 copy-start.7
  584.2 1.9 copy-start.7
  608.3 1.9 copy-start.7
  632.4 1.9 copy-start.7
  656.5 1.9 copy-start.7
  680.6 1.9 copy-start.7
  704.7 1.9 copy-start.7
  728.7 1.9 copy-start.7
  752.8 1.9 copy-start.7
  776.9 1.9 copy-start.7
  801.0 1.9 copy-start.7
  828.8 5.1 copy-start.3
  828.8 189.1 %copy-start.6 = (f32[24]{0:T(128)S(1)}, f32[24]{0:T(128)}, u32[]{:S(2)}) copy-start(f32[24]{0:T(128)} %param.19) | copy-start | bytes 292
Sparse Core Ops, SparseCore 0:
  835.7 339.2 all-reduce.3
